TPU v7x, 512 devices: a whole 4x8x8 slice. The times are simulated.
512 devices in a mesh: patch: 64 (over y, z), visit: 8 (over x, core).
Axes of the slice: x: 4, y: 8, z: 8, core: 2. Of those that a mesh axis runs over, the one named last changes fastest.
Arguments:
- stamps: bfloat16 [8, 8192, 32, 128], P('visit', 'patch'), may hold values from -6 to 6
- coefs: bfloat16 [8, 8192, 64], P('visit', 'patch'), may hold values from -0.75 to 0.75
- basis: bfloat16 [8, 64, 21, 21], P('visit', 'patch'), may hold values from -0.29882812 to 0.29882812
- taps: bfloat16 [8, 8192, 8], P('visit', 'patch'), may hold values from 0.049804688 to 0.59765625
- weights: bfloat16 [8, 8192], P('visit', 'patch'), may hold values from 0.19921875 to 5
- target: int32 [8, 8192, 1], P('visit', 'patch'), may hold values from 0 to 63; in each aligned block of 128 rows (0 to 127, 128 to 255, ..., all dimensions but the last counted through in order) at most 4 rows name the same one
- row_offset: int32 [8, 8192], P('visit', 'patch'), may hold values from 0 to 223
- col_offset: int32 [8, 8192], P('visit', 'patch'), may hold values from 0 to 127
Outputs:
- coadd: float32 [64, 256, 256], P('patch', 'visit')
- depth_map: float32 [64, 256, 256], P('patch', 'visit')
Inputs may be any that keep to these rules, and one draw needn't show every extreme that they name: `target`: among the rows of one device no patch is named more than 4 times, a bound that some block reaches.
All inputs are finite; a program needn't handle non-finite values.
Results may differ from a plain program's by a relative error of at most 0.0057.
Values may be sent and summed in bfloat16 or wider, within the bound.
No kernel may reach another device: no remote copies, remote signals or barrier semaphores. Data moves between devices by JAX's collectives and lax.ppermute only.
A program may use at most 64 MiB of HBM per device.

v0:
```python
import jax
import jax.numpy as jnp
from jax import lax
from jax.sharding import PartitionSpec as P

PATCH_ROWS = 256
PATCH_COLS = 256


def make_kernels(coefficients, basis_set):
    term_count = basis_set.shape[0]
    kernel_size = basis_set.shape[1]
    flat = jnp.dot(
        coefficients,
        basis_set.reshape(term_count, kernel_size * kernel_size),
        preferred_element_type=jnp.float32,
    )
    return flat.astype(jnp.bfloat16).reshape(coefficients.shape[0], kernel_size, kernel_size)


def convolve(pixels, kernels):
    kernel_size = kernels.shape[1]
    kernel_reach = kernel_size // 2
    height = pixels.shape[1]
    breadth = pixels.shape[2]
    padded = jnp.pad(pixels, ((0, 0), (0, 0), (kernel_reach, kernel_reach)))
    shifted = jnp.stack(
        [
            padded[:, :, column_shift : column_shift + breadth]
            for column_shift in range(kernel_size)
        ],
        axis=1,
    )
    offsets = (
        jnp.arange(height, dtype=jnp.int32)[None, :]
        - jnp.arange(height, dtype=jnp.int32)[:, None]
        + kernel_reach
    )
    onehot = (
        offsets[None, :, :] == jnp.arange(kernel_size, dtype=jnp.int32)[:, None, None]
    ).astype(jnp.bfloat16)
    toeplitz = jnp.einsum(
        "nab,aij->nbij", kernels, onehot, preferred_element_type=jnp.float32
    ).astype(jnp.bfloat16)
    result = jnp.einsum("nbik,nbkj->nij", toeplitz, shifted, preferred_element_type=jnp.float32)
    return result.astype(jnp.bfloat16)


def resample(convolved, tap_values, scale, row_start, col_start):
    height = convolved.shape[1]
    breadth = convolved.shape[2]
    column_gap = (
        jnp.arange(PATCH_COLS, dtype=jnp.int32)[None, :, None]
        - col_start[:, None, None]
        - jnp.arange(breadth, dtype=jnp.int32)[None, None, :]
        + 1
    )
    row_gap = (
        jnp.arange(PATCH_ROWS, dtype=jnp.int32)[None, :, None]
        - row_start[:, None, None]
        - jnp.arange(height, dtype=jnp.int32)[None, None, :]
        + 1
    )
    column_sum = jnp.zeros(column_gap.shape, jnp.float32)
    row_sum = jnp.zeros(row_gap.shape, jnp.float32)
    for tap_index in range(4):
        column_sum = column_sum + jnp.where(
            column_gap == tap_index,
            tap_values[:, 4 + tap_index].astype(jnp.float32)[:, None, None],
            0.0,
        )
        row_sum = row_sum + jnp.where(
            row_gap == tap_index, tap_values[:, tap_index].astype(jnp.float32)[:, None, None], 0.0
        )
    column_map = column_sum.astype(jnp.bfloat16)
    row_map = (scale.astype(jnp.float32)[:, None, None] * row_sum).astype(jnp.bfloat16)
    spread = jnp.einsum(
        "nij,ncj->nic", convolved, column_map, preferred_element_type=jnp.float32
    ).astype(jnp.bfloat16)
    return (row_map, column_map, spread)


def accumulate(pixels, extras, starts, full_basis):
    block_size = 8
    block_count = pixels.shape[0] // block_size
    term_count = full_basis.shape[0]
    blocks = (
        pixels.reshape(block_count, block_size, pixels.shape[1], pixels.shape[2]),
        extras.reshape(block_count, block_size, extras.shape[1]),
        starts.reshape(block_count, block_size, 2),
    )

    def update(state, block):
        numerator, depth_map = state
        convolved, extra_block, start_block = block
        convolved = convolve(convolved, make_kernels(extra_block[:, :term_count], full_basis))
        extra_block = extra_block[:, term_count:]
        row_map, column_map, spread = resample(
            convolved, extra_block[:, :8], extra_block[:, 8], start_block[:, 0], start_block[:, 1]
        )
        numerator = numerator + jnp.einsum(
            "nri,nic->rc", row_map, spread, preferred_element_type=jnp.float32
        )
        row_weight = jnp.sum(row_map.astype(jnp.float32), axis=2)
        column_weight = jnp.sum(column_map.astype(jnp.float32), axis=2)
        depth_map = depth_map + jnp.dot(
            row_weight.T, column_weight, precision=lax.Precision.HIGHEST
        )
        return ((numerator, depth_map), None)

    initial = (
        jnp.zeros((PATCH_ROWS, PATCH_COLS), jnp.float32),
        jnp.zeros((PATCH_ROWS, PATCH_COLS), jnp.float32),
    )
    final_state, unused = lax.scan(update, initial, blocks)
    return final_state


def per_device(stamps, coefs, basis, taps, weights, target, row_offset, col_offset):
    peer_count = lax.axis_size("patch")
    stamp_count = stamps.shape[1]
    height = stamps.shape[2]
    breadth = stamps.shape[3]
    slot_count = 2 * stamp_count // peer_count
    full_basis = lax.all_gather(basis[0], "patch", axis=0, tiled=True)
    destination = target[0, :, 0]
    position = jnp.arange(stamp_count, dtype=jnp.int32)
    earlier = (destination[None, :] == destination[:, None]) & (
        position[None, :] < position[:, None]
    )
    standing = jnp.sum(earlier.astype(jnp.int32), axis=1)
    placement = destination * slot_count + standing
    chooser = placement[None, :] == jnp.arange(peer_count * slot_count, dtype=jnp.int32)[:, None]
    select = chooser.astype(jnp.bfloat16)

    def pack(values):
        packed = jnp.dot(select, values, preferred_element_type=jnp.float32).astype(jnp.bfloat16)
        return packed.reshape(peer_count, slot_count, values.shape[1])

    starts = jnp.stack([row_offset[0], col_offset[0]], axis=1)
    packed_starts = jnp.sum(jnp.where(chooser[:, :, None], starts[None, :, :], 0), axis=1).reshape(
        peer_count, slot_count, 2
    )
    total_slots = peer_count * slot_count
    extras = jnp.concatenate([coefs[0], taps[0], weights[0][:, None]], axis=1)
    packed_pixels = pack(stamps[0].reshape(stamp_count, height * breadth))
    packed_extras = pack(extras)
    got_pixels, got_extras, got_starts = (
        lax.all_to_all(packed_pixels, "patch", split_axis=0, concat_axis=0, tiled=True),
        lax.all_to_all(packed_extras, "patch", split_axis=0, concat_axis=0, tiled=True),
        lax.all_to_all(packed_starts, "patch", split_axis=0, concat_axis=0, tiled=True),
    )
    numerator, depth_map = accumulate(
        got_pixels.reshape(total_slots, height, breadth),
        got_extras.reshape(total_slots, got_extras.shape[2]),
        got_starts.reshape(total_slots, 2),
        full_basis,
    )
    numerator, depth_map = (
        lax.psum_scatter(numerator, "visit", scatter_dimension=0, tiled=True),
        lax.psum_scatter(depth_map, "visit", scatter_dimension=0, tiled=True),
    )
    coadd = numerator / (1.0 + depth_map)
    return (coadd[None], depth_map[None])


def solution(mesh):
    placed = (
        P("visit", "patch", None, None),
        P("visit", "patch", None),
        P("visit", "patch", None, None),
        P("visit", "patch", None),
        P("visit", "patch"),
        P("visit", "patch", None),
        P("visit", "patch"),
        P("visit", "patch"),
    )
    return jax.shard_map(
        per_device,
        mesh=mesh,
        in_specs=placed,
        out_specs=(P("patch", "visit", None), P("patch", "visit", None)),
        check_vma=False,
    )
```

profile of v0, /device:TPU:8, one launch (start us, length us, event | category | flops | bytes accessed | tf_op | source)
XLA Modules:
  0.0 502.9 jit_solution(15867285318595806077)
XLA Ops:
  7.2 0.9 convert_reduce_fusion.2
  10.4 16.6 %all-to-all-start.1 = ((s32[64,4,2]{1,2,0:T(2,128)}), s32[64,4,2]{1,2,0:T(2,128)S(1)}, u32[]{:S(2)}, u32[]{:S(2)}) async-start(s32[64,4,2]{1,2,0:T(2,128)} %copy.93), calls=%async_computation.1 | async-start | bytes 131072 | tf_op jit(solution)/shard_map/all_to_all | solution.py:151
  27.0 2.0 convolution_convert_fusion.3
  28.9 2.2 reshape.221
  31.2 7.1 %all-to-all-done.1 = s32[64,4,2]{1,2,0:T(2,128)S(1)} async-done(((s32[64,4,2]{1,2,0:T(2,128)}), s32[64,4,2]{1,2,0:T(2,128)S(1)}, u32[]{:S(2)}, u32[]{:S(2)}) %all-to-all-start.1) | async-done | bytes 2080 | tf_op jit(solution)/shard_map/all_to_all | solution.py:151
  38.3 5.7 %all-to-all-start.2 = ((bf16[64,4,4096]{2,1,0:T(4,128)(2,1)}), bf16[64,4,4096]{2,1,0:T(4,128)(2,1)S(1)}, u32[]{:S(2)}, u32[]{:S(2)}) async-start(bf16[64,4,4096]{2,1,0:T(4,128)(2,1)} %reshape.221), calls=%async_computation.2 | async-start | bytes 4194304 | tf_op jit(solution)/shard_map/all_to_all | solution.py:149
  45.0 50.3 %all-to-all-done.2 = bf16[64,4,4096]{2,1,0:T(4,128)(2,1)S(1)} async-done(((bf16[64,4,4096]{2,1,0:T(4,128)(2,1)}), bf16[64,4,4096]{2,1,0:T(4,128)(2,1)S(1)}, u32[]{:S(2)}, u32[]{:S(2)}) %all-to-all-start.2) | async-done | bytes 2097184 | tf_op jit(solution)/shard_map/all_to_all | solution.py:149
  95.3 12.5 %all-to-all-start = ((bf16[64,4,73]{2,1,0:T(4,128)(2,1)}), bf16[64,4,73]{2,1,0:T(4,128)(2,1)S(1)}, u32[]{:S(2)}, u32[]{:S(2)}) async-start(bf16[64,4,73]{2,1,0:T(4,128)(2,1)} %bitcast.4), calls=%async_computation | async-start | bytes 131072 | tf_op jit(solution)/shard_map/all_to_all | solution.py:150
  107.9 49.5 %all-gather = bf16[64,1,21,21]{3,2,1,0:T(8,128)(2,1)S(1)} all-gather(bf16[1,1,21,21]{3,2,1,0:T(8,128)(2,1)S(1)} %copy-done.3), channel_id=2, replica_groups=mesh['patch'=64,'visit'=8] {'patch'}, dimensions={0}, use_global_device_ids=true | all-gather | bytes 57330 | tf_op jit(solution)/shard_map/all_gather | solution.py:125
  157.8 3.2 reshape_reshape.11
  161.0 261.2 %while.16 = (s32[]{:T(128)}, f32[256,256]{1,0:T(8,128)S(1)}, f32[256,256]{1,0:T(8,128)S(1)}, bf16[32,8,73]{2,1,0:T(8,128)(2,1)S(1)}, s32[32,8,2]{1,0,2:T(8,128)S...) while((s32[]{:T(128)}, f32[256,256]{1,0:T(8,128)S(1)}, ...), condition=%wide.wide.region_5.6_spmd.clone, body=%wide.wide.region_2.5_spmd.clone.sunk | while | flops 118861328 | bytes 6383152 | solution.py:115
  166.6 0.9 fusion.192
  174.8 0.9 fusion.192
  182.9 0.9 fusion.192
  199.3 0.9 fusion.192
  215.6 0.9 fusion.192
  231.9 0.9 fusion.192
  248.2 0.9 fusion.192
  264.6 0.9 fusion.192
  280.9 0.9 fusion.192
  297.2 0.9 fusion.192
  313.6 0.9 fusion.192
  321.7 0.9 fusion.192
  329.9 0.9 fusion.192
  346.2 0.9 fusion.192
  362.5 0.9 fusion.192
  378.9 0.9 fusion.192
  395.2 0.9 fusion.192
  411.5 0.9 fusion.192
  423.7 33.2 %reduce-scatter.5.cloned.1.call-done = f32[32,256]{1,0:T(8,128)} async-done(((f32[256,256]{1,0:T(8,128)}), f32[32,256]{1,0:T(8,128)}) %reduce-scatter.5.cloned.1.call-update) | async-done | bytes 32784 | tf_op jit(solution)/shard_map/reduce_scatter | solution.py:161
  456.9 37.8 %reduce-scatter.3.cloned.1.call-done = f32[32,256]{1,0:T(8,128)} async-done(((f32[256,256]{1,0:T(8,128)}), f32[32,256]{1,0:T(8,128)}) %reduce-scatter.3.cloned.1.call-update) | async-done | bytes 32784 | tf_op jit(solution)/shard_map/reduce_scatter | solution.py:160
  494.7 1.4 divide_bitcast_fusion
  (1199 shorter events, 244.5 us)
Async XLA Ops:
  10.4 27.9 %all-to-all-start.1 = ((s32[64,4,2]{1,2,0:T(2,128)}), s32[64,4,2]{1,2,0:T(2,128)S(1)}, u32[]{:S(2)}, u32[]{:S(2)}) async-start(s32[64,4,2]{1,2,0:T(2,128)} %copy.93), calls=%async_computation.1 | async-start | bytes 131072 | tf_op jit(solution)/shard_map/all_to_all | solution.py:151
  31.2 12.9 %copy-start.4 = (bf16[1,128,64]{1,2,0:T(8,128)(2,1)S(1)}, bf16[1,128,64]{1,2,0:T(8,128)(2,1)}, u32[]{:S(2)}) copy-start(bf16[1,128,64]{1,2,0:T(8,128)(2,1)} %param.11) | copy-start | bytes 49156
  31.2 12.9 %copy-start.5 = (bf16[1,128,8]{1,2,0:T(8,128)(2,1)S(1)}, bf16[1,128,8]{1,2,0:T(8,128)(2,1)}, u32[]{:S(2)}) copy-start(bf16[1,128,8]{1,2,0:T(8,128)(2,1)} %param.13) | copy-start | bytes 6148
  31.2 12.9 %copy-start.6 = (bf16[1,128]{1,0:T(2,128)(2,1)S(1)}, bf16[1,128]{1,0:T(2,128)(2,1)}, u32[]{:S(2)}) copy-start(bf16[1,128]{1,0:T(2,128)(2,1)} %param.14) | copy-start | bytes 772
  31.2 76.7 %copy-start.3 = (bf16[1,1,21,21]{3,2,1,0:T(8,128)(2,1)S(1)}, bf16[1,1,21,21]{3,2,1,0:T(8,128)(2,1)}, u32[]{:S(2)}) copy-start(bf16[1,1,21,21]{3,2,1,0:T(8,128)(2,1)} %param.12) | copy-start | bytes 2650
  38.3 57.0 %all-to-all-start.2 = ((bf16[64,4,4096]{2,1,0:T(4,128)(2,1)}), bf16[64,4,4096]{2,1,0:T(4,128)(2,1)S(1)}, u32[]{:S(2)}, u32[]{:S(2)}) async-start(bf16[64,4,4096]{2,1,0:T(4,128)(2,1)} %reshape.221), calls=%async_computation.2 | async-start | bytes 4194304 | tf_op jit(solution)/shard_map/all_to_all | solution.py:149
  95.3 65.7 %all-to-all-start = ((bf16[64,4,73]{2,1,0:T(4,128)(2,1)}), bf16[64,4,73]{2,1,0:T(4,128)(2,1)S(1)}, u32[]{:S(2)}, u32[]{:S(2)}) async-start(bf16[64,4,73]{2,1,0:T(4,128)(2,1)} %bitcast.4), calls=%async_computation | async-start | bytes 131072 | tf_op jit(solution)/shard_map/all_to_all | solution.py:150
  107.8 349.1 %reduce-scatter.5.cloned.1.call-start = ((), (), s32[]{:S(2)}) async-start(), calls=%async_computation.6 | async-start | bytes 294912 | tf_op jit(solution)/shard_map/reduce_scatter | solution.py:161
  157.6 3.4 copy-start.1
  422.3 0.7 copy-start
  422.3 0.8 copy-start.2
  423.0 71.7 %reduce-scatter.3.cloned.1.call-start = ((), (), s32[]{:S(2)}) async-start(), calls=%async_computation.5 | async-start | bytes 294912 | tf_op jit(solution)/shard_map/reduce_scatter | solution.py:160
Sparse Core Ops, SparseCore 0:
  423.1 33.7 reduce-scatter.4
  459.9 34.7 reduce-scatter.2
where the time goes:
time: 506 us; the launch traced here: 503 us
  local copies, waits for them, and re-layouts  135 us (27%)
  waiting for transfers between devices  129 us (25%)
  matrix products  91.7 us (18%)
  blocking collectives  49.5 us (10%)
  other arithmetic  42.5 us (8%)
  starting transfers between devices  34.9 us (7%)
  between operations  14.2 us (3%)
  loops' own time  5.66 us (1%)
    while x640, local copies, waits for them, and re-layouts  88.1 us
    all_to_all x1, waiting for transfers between devices, per_device(): lax.all_to_all(packed_pixels, 'patch', split_axis=0, concat_axis=0, tiled...  50.3 us
    all_gather x1, blocking collectives, per_device(): full_basis = lax.all_gather(basis[0], 'patch', axis=0, tiled=True)  49.5 us
    reduce_scatter x1, waiting for transfers between devices, per_device(): lax.psum_scatter(numerator, 'visit', scatter_dimension=0, tiled=True)  37.8 us
    reduce_scatter x1, waiting for transfers between devices, per_device(): lax.psum_scatter(depth_map, 'visit', scatter_dimension=0, tiled=True)  33.2 us
    dot_general x32, matrix products, update(): jnp.einsum('nri,nic->rc', row_map, spread, preferred_element_type=jnp.flo...  28.8 us
    reduce_sum x32, other arithmetic, update(): column_weight = jnp.sum(column_map.astype(jnp.float32), axis=2)  27.4 us
    squeeze x32, local copies, waits for them, and re-layouts, accumulate(): final_state, unused = lax.scan(update, initial, blocks)  27.1 us
  transfers between devices with their start and end apart: 5, of which 4 were waited for; matrix products, arithmetic and copies ran while one was open for 2% of the time, Pallas kernels for 0%

commit v1 on v0

--- a/solution.py
+++ b/solution.py
@@ -122,7 +122,8 @@
     height = stamps.shape[2]
     breadth = stamps.shape[3]
     slot_count = 2 * stamp_count // peer_count
-    full_basis = lax.all_gather(basis[0], "patch", axis=0, tiled=True)
+    copies = jnp.concatenate([basis[0]] * lax.axis_size("patch"), axis=0)
+    full_basis = lax.all_to_all(copies, "patch", 0, 0, tiled=True)
     destination = target[0, :, 0]
     position = jnp.arange(stamp_count, dtype=jnp.int32)
     earlier = (destination[None, :] == destination[:, None]) & (

time: 506 us -> 481 us (0.951)
  blocking collectives: 49.5 us -> 27.7 us
  starting transfers between devices: 34.9 us -> 24.4 us
  waiting for transfers between devices: 129 us -> 135 us
    all_gather x1 -> x0, blocking collectives: 49.5 us -> none  [per_device(): full_basis = lax.all_gather(basis[0], 'patch', axis=0, tiled=True)]
    all_to_all x0 -> x1, blocking collectives: none -> 27.7 us  [per_device(): lax.all_to_all(packed_starts, 'patch', split_axis=0, concat_axis=0, tiled...]
    all_to_all x1, starting transfers between devices: 16.6 us -> 5.53 us  [per_device(): full_basis = lax.all_to_all(copies, 'patch', 0, 0, tiled=True)]
    all_to_all x1, waiting for transfers between devices: 0.01 us -> 7.61 us  [per_device(): lax.all_to_all(packed_extras, 'patch', split_axis=0, concat_axis=0, tiled...]
  transfers between devices with their start and end apart: 5 -> 5, of which waited for: 4 -> 5; matrix products, arithmetic and copies ran while one was open for 2% -> 2% of each run, Pallas kernels for 0% -> 0%
where the time goes in v1:
time: 481 us; the launch traced here: 477 us
  local copies, waits for them, and re-layouts  136 us (28%)
  waiting for transfers between devices  135 us (28%)
  matrix products  91.7 us (19%)
  other arithmetic  42.5 us (9%)
  blocking collectives  27.7 us (6%)
  starting transfers between devices  24.4 us (5%)
  between operations  14.2 us (3%)
  loops' own time  5.66 us (1%)
    while x640, local copies, waits for them, and re-layouts  88.1 us
    all_to_all x1, waiting for transfers between devices, per_device(): lax.all_to_all(packed_pixels, 'patch', split_axis=0, concat_axis=0, tiled...  49.8 us
    reduce_scatter x1, waiting for transfers between devices, per_device(): lax.psum_scatter(numerator, 'visit', scatter_dimension=0, tiled=True)  37.8 us
    dot_general x32, matrix products, update(): jnp.einsum('nri,nic->rc', row_map, spread, preferred_element_type=jnp.flo...  28.8 us
    reduce_scatter x1, waiting for transfers between devices, per_device(): lax.psum_scatter(depth_map, 'visit', scatter_dimension=0, tiled=True)  28.3 us
    all_to_all x1, blocking collectives, per_device(): lax.all_to_all(packed_starts, 'patch', split_axis=0, concat_axis=0, tiled...  27.7 us
    reduce_sum x32, other arithmetic, update(): column_weight = jnp.sum(column_map.astype(jnp.float32), axis=2)  27.4 us
    squeeze x32, local copies, waits for them, and re-layouts, accumulate(): final_state, unused = lax.scan(update, initial, blocks)  27.1 us
  transfers between devices with their start and end apart: 5, of which 5 were waited for; matrix products, arithmetic and copies ran while one was open for 2% of the time, Pallas kernels for 0%

profile of v1, /device:TPU:8, one launch (start us, length us, event | category | flops | bytes accessed | tf_op | source)
XLA Modules:
  0.0 477.1 jit_solution(18073246285722644775)
XLA Ops:
  7.2 0.9 convert_reduce_fusion.2
  9.8 27.7 %all_to_all.20 = s32[64,4,2]{1,2,0:T(2,128)S(1)} all-to-all(s32[64,4,2]{1,2,0:T(2,128)S(1)} %copy.90), channel_id=1, replica_groups=mesh['patch'=64,'visit'=8] {'patch'}, dimensions={0} | all-to-all | bytes 4096 | tf_op jit(solution)/shard_map/all_to_all | solution.py:152
  37.5 1.5 concatenate.7
  38.9 5.5 %all-to-all-start.2 = ((bf16[64,21,21]{2,1,0:T(8,128)(2,1)}), bf16[64,21,21]{2,1,0:T(8,128)(2,1)S(1)}, u32[]{:S(2)}, u32[]{:S(2)}) async-start(bf16[64,21,21]{2,1,0:T(8,128)(2,1)} %concatenate.7), calls=%async_computation.2 | async-start | bytes 786432 | tf_op jit(solution)/shard_map/all_to_all | solution.py:126
  44.5 2.0 convolution_convert_fusion.3
  46.4 2.2 reshape.223
  48.7 10.6 %all-to-all-done.2 = bf16[64,21,21]{2,1,0:T(8,128)(2,1)S(1)} async-done(((bf16[64,21,21]{2,1,0:T(8,128)(2,1)}), bf16[64,21,21]{2,1,0:T(8,128)(2,1)S(1)}, u32[]{:S(2)}, u32[]{:S(2)}) %all-to-all-start.2) | async-done | bytes 56480 | tf_op jit(solution)/shard_map/all_to_all | solution.py:126
  59.3 6.0 %all-to-all-start.3 = ((bf16[64,4,4096]{2,1,0:T(4,128)(2,1)}), bf16[64,4,4096]{2,1,0:T(4,128)(2,1)S(1)}, u32[]{:S(2)}, u32[]{:S(2)}) async-start(bf16[64,4,4096]{2,1,0:T(4,128)(2,1)} %reshape.223), calls=%async_computation.3 | async-start | bytes 4194304 | tf_op jit(solution)/shard_map/all_to_all | solution.py:150
  66.2 49.8 %all-to-all-done.3 = bf16[64,4,4096]{2,1,0:T(4,128)(2,1)S(1)} async-done(((bf16[64,4,4096]{2,1,0:T(4,128)(2,1)}), bf16[64,4,4096]{2,1,0:T(4,128)(2,1)S(1)}, u32[]{:S(2)}, u32[]{:S(2)}) %all-to-all-start.3) | async-done | bytes 2097184 | tf_op jit(solution)/shard_map/all_to_all | solution.py:150
  116.0 12.7 %all-to-all-start = ((bf16[64,4,73]{2,1,0:T(4,128)(2,1)}), bf16[64,4,73]{2,1,0:T(4,128)(2,1)S(1)}, u32[]{:S(2)}, u32[]{:S(2)}) async-start(bf16[64,4,73]{2,1,0:T(4,128)(2,1)} %bitcast.4), calls=%async_computation | async-start | bytes 131072 | tf_op jit(solution)/shard_map/all_to_all | solution.py:151
  129.2 3.2 reshape_reshape.11
  132.5 7.6 %all-to-all-done = bf16[64,4,73]{2,1,0:T(4,128)(2,1)S(1)} async-done(((bf16[64,4,73]{2,1,0:T(4,128)(2,1)}), bf16[64,4,73]{2,1,0:T(4,128)(2,1)S(1)}, u32[]{:S(2)}, u32[]{:S(2)}) %all-to-all-start) | async-done | bytes 37408 | tf_op jit(solution)/shard_map/all_to_all | solution.py:151
  140.1 261.2 %while.16 = (s32[]{:T(128)}, f32[256,256]{1,0:T(8,128)S(1)}, f32[256,256]{1,0:T(8,128)S(1)}, bf16[32,8,73]{2,1,0:T(8,128)(2,1)S(1)}, s32[32,8,2]{1,0,2:T(8,128)S...) while((s32[]{:T(128)}, f32[256,256]{1,0:T(8,128)S(1)}, ...), condition=%wide.wide.region_5.6_spmd.clone, body=%wide.wide.region_2.5_spmd.clone.sunk | while | flops 118861328 | bytes 6383152 | solution.py:115
  153.8 0.9 fusion.192
  170.2 0.9 fusion.192
  186.5 0.9 fusion.192
  202.8 0.9 fusion.192
  219.2 0.9 fusion.192
  235.5 0.9 fusion.192
  251.8 0.9 fusion.192
  268.1 0.9 fusion.192
  284.5 0.9 fusion.192
  300.8 0.9 fusion.192
  317.1 0.9 fusion.192
  333.5 0.9 fusion.192
  349.8 0.9 fusion.192
  366.1 0.9 fusion.192
  382.4 0.9 fusion.192
  398.8 0.9 fusion.192
  402.8 28.3 %reduce-scatter.5.cloned.1.call-done = f32[32,256]{1,0:T(8,128)} async-done(((f32[256,256]{1,0:T(8,128)}), f32[32,256]{1,0:T(8,128)}) %reduce-scatter.5.cloned.1.call-update) | async-done | bytes 32784 | tf_op jit(solution)/shard_map/reduce_scatter | solution.py:162
  431.1 37.8 %reduce-scatter.3.cloned.1.call-done = f32[32,256]{1,0:T(8,128)} async-done(((f32[256,256]{1,0:T(8,128)}), f32[32,256]{1,0:T(8,128)}) %reduce-scatter.3.cloned.1.call-update) | async-done | bytes 32784 | tf_op jit(solution)/shard_map/reduce_scatter | solution.py:161
  468.9 1.4 divide_bitcast_fusion
  (1198 shorter events, 245.7 us)
Async XLA Ops:
  38.9 20.3 %all-to-all-start.2 = ((bf16[64,21,21]{2,1,0:T(8,128)(2,1)}), bf16[64,21,21]{2,1,0:T(8,128)(2,1)S(1)}, u32[]{:S(2)}, u32[]{:S(2)}) async-start(bf16[64,21,21]{2,1,0:T(8,128)(2,1)} %concatenate.7), calls=%async_computation.2 | async-start | bytes 786432 | tf_op jit(solution)/shard_map/all_to_all | solution.py:126
  48.7 16.6 %copy-start.3 = (bf16[1,128,64]{1,2,0:T(8,128)(2,1)S(1)}, bf16[1,128,64]{1,2,0:T(8,128)(2,1)}, u32[]{:S(2)}) copy-start(bf16[1,128,64]{1,2,0:T(8,128)(2,1)} %param.11) | copy-start | bytes 49156
  48.7 16.6 %copy-start.4 = (bf16[1,128,8]{1,2,0:T(8,128)(2,1)S(1)}, bf16[1,128,8]{1,2,0:T(8,128)(2,1)}, u32[]{:S(2)}) copy-start(bf16[1,128,8]{1,2,0:T(8,128)(2,1)} %param.13) | copy-start | bytes 6148
  48.7 16.6 %copy-start.5 = (bf16[1,128]{1,0:T(2,128)(2,1)S(1)}, bf16[1,128]{1,0:T(2,128)(2,1)}, u32[]{:S(2)}) copy-start(bf16[1,128]{1,0:T(2,128)(2,1)} %param.14) | copy-start | bytes 772
  59.3 56.7 %all-to-all-start.3 = ((bf16[64,4,4096]{2,1,0:T(4,128)(2,1)}), bf16[64,4,4096]{2,1,0:T(4,128)(2,1)S(1)}, u32[]{:S(2)}, u32[]{:S(2)}) async-start(bf16[64,4,4096]{2,1,0:T(4,128)(2,1)} %reshape.223), calls=%async_computation.3 | async-start | bytes 4194304 | tf_op jit(solution)/shard_map/all_to_all | solution.py:150
  116.0 24.1 %all-to-all-start = ((bf16[64,4,73]{2,1,0:T(4,128)(2,1)}), bf16[64,4,73]{2,1,0:T(4,128)(2,1)S(1)}, u32[]{:S(2)}, u32[]{:S(2)}) async-start(bf16[64,4,73]{2,1,0:T(4,128)(2,1)} %bitcast.4), calls=%async_computation | async-start | bytes 131072 | tf_op jit(solution)/shard_map/all_to_all | solution.py:151
  128.7 302.4 %reduce-scatter.5.cloned.1.call-start = ((), (), s32[]{:S(2)}) async-start(), calls=%async_computation.7 | async-start | bytes 294912 | tf_op jit(solution)/shard_map/reduce_scatter | solution.py:162
  129.2 3.3 copy-start.1
  401.3 0.7 copy-start
  401.4 0.8 copy-start.2
  402.1 66.8 %reduce-scatter.3.cloned.1.call-start = ((), (), s32[]{:S(2)}) async-start(), calls=%async_computation.6 | async-start | bytes 294912 | tf_op jit(solution)/shard_map/reduce_scatter | solution.py:161
Sparse Core Ops, SparseCore 0:
  402.2 28.8 reduce-scatter.4
  434.1 34.7 reduce-scatter.2
